TPU v7x, 256 devices: a whole 4x4x8 slice. The times are simulated.
256 devices in a mesh: section: 128 (over z, y, x), attn: 2 (over core).
Axes of the slice: x: 4, y: 4, z: 8, core: 2. Of those that a mesh axis runs over, the one named last changes fastest.
Arguments:
- queries: bfloat16 [65536, 3072], P(('section', 'attn')), may hold values from -120 to 120
- keys: bfloat16 [65536, 1024], P(('section', 'attn')), may hold values from -2.5 to 2.5
- values: bfloat16 [65536, 1024], P(('section', 'attn')), may hold values from -4 to 4
- doc_ids: int32 [65536], replicated, may hold values from 0 to 127, never falling along the last dimension, each value on 1 to 1792 neighbouring positions
Outputs:
- attended: bfloat16 [65536, 3072], P(('section', 'attn'))
Inputs may be any that keep to these rules, and one draw needn't show every extreme that they name: `doc_ids`: along the pack the document numbers never fall, and a document holds at most 1792 tokens.
All inputs are finite; a program needn't handle non-finite values.
Results may differ from a plain program's by a relative error of at most 0.0028.
Values may be sent and summed in bfloat16 or wider, within the bound.
A program may use at most 64 MiB of HBM per device.

v0:
```python
import functools
import math

import jax
import jax.numpy as jnp
from jax import lax
from jax.experimental import pallas as pl
from jax.experimental.pallas import tpu as pltpu
from jax.sharding import PartitionSpec as P

MESH = pl.DeviceIdType.MESH
HEAD_DIM = 128
GROUP = 3
RING = 4
LANES = 128
NEG = -1e30

OWN, EXTRA, BACK1, BACK2, BACK3, RELAY = 0, 1, 2, 4, 6, 8
BLOCKS = 9
UP, RIGHT, LEFT, NEXT, PREV, SIDE_EXTRA, SIDE1, SIDE2, SIDE3 = range(9)
KINDS = 9


def attention_kernel(
    sections, rows, heads,
    q_hbm, k_hbm, v_hbm, docs_hbm, out_hbm,
    kv, q, onehot, away, docs, stat_max, acc, out,
    send_sem, recv_sem, q_sem, kv_sem, doc_sem, out_sem,
):
    half = heads // 2
    scale = math.log2(math.e) * HEAD_DIM ** (-0.5)
    s = lax.axis_index("section")
    c = lax.axis_index("attn")
    x = lax.rem(s, RING)
    row_start = s - x
    first, last = x == 0, x == RING - 1
    edge = jnp.logical_or(first, last)

    right = row_start + lax.rem(x + 1, RING)
    left = row_start + lax.rem(x + RING - 1, RING)
    up = lax.rem(s + RING, sections)
    down = lax.rem(s + sections - RING, sections)
    following = lax.rem(s + 1, sections)
    previous = lax.rem(s + sections - 1, sections)
    other = 1 - c
    up_core = jnp.where(first, other, c)

    def load_kv(j):
        at = pl.ds(pl.multiple_of(j * HEAD_DIM, HEAD_DIM), HEAD_DIM)
        return (
            pltpu.make_async_copy(k_hbm.at[:, at], kv.at[OWN, j, 0], kv_sem.at[0, j]),
            pltpu.make_async_copy(v_hbm.at[:, at], kv.at[OWN, j, 1], kv_sem.at[1, j]),
        )

    def load_q(h):
        at = pl.ds(pl.multiple_of(h * HEAD_DIM, HEAD_DIM), HEAD_DIM)
        return pltpu.make_async_copy(q_hbm.at[:, at], q.at[h], q_sem.at[h])

    def load_docs(piece):
        pair = lax.rem(lax.div(s, 2) + sections // 2 - 2 + piece, sections // 2)
        return pltpu.make_async_copy(
            docs_hbm.at[pl.ds(pl.multiple_of(pair * 8, 8), 8), :],
            docs.at[pl.ds(piece * 8, 8), :],
            doc_sem.at[piece],
        )

    @pl.loop(0, heads)
    def _(j):
        for copy in load_kv(j):
            copy.start()

    for piece in range(3):
        load_docs(piece).start()

    barrier = pltpu.get_barrier_semaphore()

    def greet(section, core):
        pl.semaphore_signal(barrier, inc=1, device_id=(section, core), device_id_type=MESH)

    greet(s, other)
    greet(right, c)
    greet(left, c)
    greet(up, up_core)
    greet(down, up_core)

    @pl.when(first)
    def _():
        greet(previous, c)

    @pl.when(last)
    def _():
        greet(following, c)

    @pl.loop(0, heads * GROUP)
    def _(h):
        load_q(h).start()

    def send(kind, j, source, target, section, core):
        return pltpu.make_async_remote_copy(
            src_ref=kv.at[source, j],
            dst_ref=kv.at[target, j],
            send_sem=send_sem.at[kind, j],
            recv_sem=recv_sem.at[target, j],
            device_id=(section, core),
            device_id_type=MESH,
        )

    def arrived(block, j):
        send(UP, j, block, block, s, other).wait_recv()

    up_target = jnp.where(first, EXTRA, RELAY)
    right_source = jnp.where(last, RELAY, OWN)
    left_source = jnp.where(first, OWN, RELAY)

    def send_up(j):
        return send(UP, j, OWN, up_target, up, up_core)

    def send_right(j):
        return send(RIGHT, j, right_source, BACK1 + c, right, c)

    def send_left(j):
        return send(LEFT, j, left_source, BACK3 + c, left, c)

    def send_next(j):
        return send(NEXT, j, BACK1 + c, BACK2 + c, following, c)

    def send_prev(j):
        return send(PREV, j, BACK3 + c, BACK2 + c, previous, c)

    def send_extra(j):
        return send(SIDE_EXTRA, j, jnp.where(c == 0, OWN, RELAY), EXTRA, s, other)

    def send_side(kind, j, block):
        return send(kind, j, block + c, block + c, s, other)

    sends_up = jnp.logical_or(x > 0, c == 1)
    sends_extra = jnp.logical_or(x > 0, c == 0)
    relays = x > 0

    @pl.loop(0, heads)
    def _(j):
        for copy in load_kv(j):
            copy.wait()

    pl.semaphore_wait(barrier, jnp.where(edge, 6, 5))

    @pl.loop(0, heads)
    def _(j):
        @pl.when(sends_up)
        def _():
            send_up(j).start()

        @pl.when(jnp.logical_not(last))
        def _():
            send_right(j).start()

        @pl.when(first)
        def _():
            send_left(j).start()

        @pl.when(c == 0)
        def _():
            send_extra(j).start()

    for piece in range(3):
        load_docs(piece).wait()
    parity = lax.rem(s, 2)
    pieces = rows // LANES
    places = ((0, c), (4 * other, other), (1, 0), (1, 1), (2, 0), (2, 1), (3, 0), (3, 1))
    ids = lax.broadcasted_iota(jnp.int32, (LANES, LANES), 0)
    for block, (back, core) in enumerate(places):
        for piece in range(pieces):
            row = (4 + parity - back) * (2 * pieces) + core * pieces + piece
            same = jnp.where(docs[pl.ds(row, 1), :] == ids, 1.0, 0.0)
            turned = jnp.transpose(same)
            onehot[block, piece * LANES:(piece + 1) * LANES, :] = turned.astype(jnp.bfloat16)
            if block == 0:
                away[piece * LANES:(piece + 1) * LANES, :] = ((1.0 - turned) * NEG).astype(jnp.bfloat16)

    @pl.loop(0, heads * GROUP)
    def _(h):
        load_q(h).wait()

    def scores(query, block, j):
        key = jnp.concatenate([kv[block, j, 0], onehot[block]], axis=1)
        return lax.dot_general(
            query, key, (((1,), (1,)), ((), ())), preferred_element_type=jnp.float32
        )

    def values_of(block, j):
        value = kv[block, j, 1]
        return jnp.concatenate([value, jnp.ones_like(value)], axis=1)

    def query_of(j, r):
        return jnp.concatenate([q[j * GROUP + r], away[...]], axis=1)

    def weigh(parts, top, blocks, j):
        total = None
        for part, block in zip(parts, blocks):
            weights = jnp.exp2((part - top) * scale).astype(jnp.bfloat16)
            product = jnp.dot(weights, values_of(block, j), preferred_element_type=jnp.float32)
            total = product if total is None else total + product
        return total

    early = (OWN, EXTRA, BACK1, BACK1 + 1, BACK3, BACK3 + 1)
    late = (BACK2, BACK2 + 1)

    def fold_early(j):
        causal = lax.broadcasted_iota(jnp.int32, (rows, rows), 1) <= lax.broadcasted_iota(
            jnp.int32, (rows, rows), 0
        )
        for r in range(GROUP):
            query = query_of(j, r)
            parts = [scores(query, block, j) for block in early]
            parts[0] = jnp.where(causal, parts[0], NEG)
            highest = functools.reduce(jnp.maximum, parts)
            top = jnp.max(highest, axis=1, keepdims=True)
            stat_max[j, r] = jnp.broadcast_to(top, (rows, LANES))
            acc[j, r] = weigh(parts, top, early, j)

    def fold_late(j):
        for r in range(GROUP):
            query = query_of(j, r)
            parts = [scores(query, block, j) for block in late]
            old = stat_max[j, r]
            highest = functools.reduce(jnp.maximum, parts)
            top = jnp.maximum(old[:, :1], jnp.max(highest, axis=1, keepdims=True))
            rescale = jnp.exp2((old[:, :1] - top) * scale)
            summed = acc[j, r] * rescale + weigh(parts, top, late, j)
            result = summed[:, :HEAD_DIM] / summed[:, HEAD_DIM:]
            out[j * GROUP + r] = result.astype(jnp.bfloat16)

    def store_out(h):
        at = pl.ds(pl.multiple_of(h * HEAD_DIM, HEAD_DIM), HEAD_DIM)
        return pltpu.make_async_copy(out.at[h], out_hbm.at[:, at], out_sem.at[h])

    shift = jnp.where(edge, 0, half)

    def pass_on(j):
        @pl.when(relays)
        def _():
            arrived(RELAY, j)
            send_left(j).start()

            @pl.when(last)
            def _():
                send_right(j).start()

            @pl.when(c == 1)
            def _():
                send_extra(j).start()

        arrived(BACK1 + c, j)
        send_side(SIDE1, j, BACK1).start()
        arrived(BACK3 + c, j)
        send_side(SIDE3, j, BACK3).start()

        @pl.when(j >= half)
        def _():
            send_next(j - shift).start()
            send_prev(j - shift).start()

    def early_ready(j):
        arrived(EXTRA, j)
        arrived(BACK1 + other, j)
        arrived(BACK3 + other, j)

    @pl.loop(0, heads + 1)
    def _(step):
        @pl.when(step < heads)
        def _():
            pass_on(step)

        @pl.when(step > 0)
        def _():
            early_ready(step - 1)
            fold_early(step - 1)

    @pl.loop(0, half)
    def _(step):
        for j in (step, step + half):
            arrived(BACK2 + c, j)
            send_side(SIDE2, j, BACK2).start()
        for j in (step, step + half):
            arrived(BACK2 + other, j)
            fold_late(j)
            for r in range(GROUP):
                store_out(j * GROUP + r).start()

    @pl.loop(0, heads)
    def _(j):
        for r in range(GROUP):
            store_out(j * GROUP + r).wait()

        @pl.when(sends_up)
        def _():
            send_up(j).wait_send()

        send_right(j).wait_send()
        send_left(j).wait_send()
        send_side(SIDE1, j, BACK1).wait_send()
        send_side(SIDE2, j, BACK2).wait_send()
        send_side(SIDE3, j, BACK3).wait_send()

        @pl.when(sends_extra)
        def _():
            send_extra(j).wait_send()

        @pl.when(j >= half)
        def _():
            send_next(j - shift).wait_send()
            send_prev(j - shift).wait_send()


def shards(sections, queries, keys, values, doc_ids):
    rows, heads = queries.shape[0], keys.shape[1] // HEAD_DIM
    docs = doc_ids.reshape(-1, LANES)
    return pl.pallas_call(
        functools.partial(attention_kernel, sections, rows, heads),
        out_shape=jax.ShapeDtypeStruct(queries.shape, jnp.bfloat16),
        in_specs=[pl.BlockSpec(memory_space=pl.ANY)] * 4,
        out_specs=pl.BlockSpec(memory_space=pl.ANY),
        scratch_shapes=[
            pltpu.VMEM((BLOCKS, heads, 2, rows, HEAD_DIM), jnp.bfloat16),
            pltpu.VMEM((heads * GROUP, rows, HEAD_DIM), jnp.bfloat16),
            pltpu.VMEM((RELAY, rows, LANES), jnp.bfloat16),
            pltpu.VMEM((rows, LANES), jnp.bfloat16),
            pltpu.VMEM((24, LANES), jnp.int32),
            pltpu.VMEM((heads, GROUP, rows, LANES), jnp.float32),
            pltpu.VMEM((heads, GROUP, rows, 2 * HEAD_DIM), jnp.float32),
            pltpu.VMEM((heads * GROUP, rows, HEAD_DIM), jnp.bfloat16),
            pltpu.SemaphoreType.DMA((KINDS, heads)),
            pltpu.SemaphoreType.DMA((BLOCKS, heads)),
            pltpu.SemaphoreType.DMA((heads * GROUP,)),
            pltpu.SemaphoreType.DMA((2, heads)),
            pltpu.SemaphoreType.DMA((3,)),
            pltpu.SemaphoreType.DMA((heads * GROUP,)),
        ],
        compiler_params=pltpu.CompilerParams(
            collective_id=0, has_side_effects=True, vmem_limit_bytes=60 * 1024 * 1024
        ),
    )(queries, keys, values, docs)


def solution(mesh):
    placed = P(("section", "attn"), None)
    return jax.shard_map(
        functools.partial(shards, mesh.shape["section"]),
        mesh=mesh,
        in_specs=(placed, placed, placed, P()),
        out_specs=placed,
        check_vma=False,
    )
```

profile of v0, /device:TPU:8, one launch (start us, length us, event | category | flops | bytes accessed | tf_op | source)
XLA Modules:
  0.0 79.6 jit_solution(12767729508563469877)
XLA Ops:
  0.0 77.0 %shard_map.46 = bf16[256,3072]{1,0:T(8,128)(2,1)} custom-call(bf16[256,3072]{1,0:T(8,128)(2,1)} %q_hbm.1, bf16[256,1024]{1,0:T(8,128)(2,1)} %k_hbm.1, bf16[256,1024]{1,0:T(8,128)(2,1)} %v_hbm.1, s32[512,128]{1,0:T(8,128)} %bitcast.1), custom_call_target="tpu_custom_call" | custom-call | tf_op jit(solution)/shard_map/pallas_call | solution.py:318
  77.0 2.7 %copy.6 = bf16[256,3072]{1,0:T(8,128)(2,1)} copy(bf16[256,3072]{1,0:T(8,128)(2,1)} %shard_map.46) | data formatting | bytes 3145728
where the time goes:
time: 79.8 us; the launch traced here: 79.6 us
  Pallas kernels  77 us (96%)
  local copies, waits for them, and re-layouts  2.65 us (3%)
    pallas_call x1, Pallas kernels, shards(): pl.pallas_call(functools.partial(attention_kernel, sections, rows, heads)...  77 us
    unnamed x1, local copies, waits for them, and re-layouts  2.65 us

commit v1 on v0

--- a/solution.py
+++ b/solution.py
@@ -35,6 +35,11 @@
     row_start = s - x
     first, last = x == 0, x == RING - 1
     edge = jnp.logical_or(first, last)
+    top, bottom = s < RING, s >= sections - RING
+    below = jnp.logical_not(top)
+    from_left = jnp.where(last, half, half + 1)
+    from_right = jnp.where(x == 1, half, half + 1)
+    wrapped = half + 1
 
     right = row_start + lax.rem(x + 1, RING)
     left = row_start + lax.rem(x + RING - 1, RING)
@@ -72,6 +77,17 @@
     for piece in range(3):
         load_docs(piece).start()
 
+    @pl.when(top)
+    def _():
+        @pl.loop(EXTRA, RELAY)
+        def _(block):
+            @pl.loop(0, heads)
+            def _(j):
+                kv[block, j] = jnp.zeros((2, rows, HEAD_DIM), kv.dtype)
+
+    up_open = jnp.logical_or(s < sections - RING, x == 1)
+    down_open = jnp.logical_or(s >= RING, x == 1)
+
     barrier = pltpu.get_barrier_semaphore()
 
     def greet(section, core):
@@ -80,8 +96,13 @@
     greet(s, other)
     greet(right, c)
     greet(left, c)
-    greet(up, up_core)
-    greet(down, up_core)
+    @pl.when(up_open)
+    def _():
+        greet(up, up_core)
+
+    @pl.when(down_open)
+    def _():
+        greet(down, up_core)
 
     @pl.when(first)
     def _():
@@ -133,20 +154,47 @@
     def send_side(kind, j, block):
         return send(kind, j, block + c, block + c, s, other)
 
-    sends_up = jnp.logical_or(x > 0, c == 1)
-    sends_extra = jnp.logical_or(x > 0, c == 0)
-    relays = x > 0
+    def both(*conditions):
+        return functools.reduce(jnp.logical_and, conditions)
+
+    def either(*conditions):
+        return functools.reduce(jnp.logical_or, conditions)
+
+    inside = jnp.logical_not(bottom)
+
+    def sends_up(j):
+        return either(both(first, c == 1, inside), both(x > 0, inside), both(x == 1, bottom, j >= wrapped))
+
+    def has_relay(j):
+        return both(x > 0, either(below, both(x == 1, j >= wrapped)))
+
+    has1 = either(below, x > 0)
+    has2 = either(below, x > 1)
+    has3 = either(below, last)
+
+    def passes3(j):
+        return both(first, top, j >= wrapped)
+
+    def has_extra():
+        return either(c == 1, below)
+
+    relays_extra = both(x > 0, below, c == 1)
+    sends_next = both(has1, jnp.logical_not(both(bottom, last)))
+    sends_prev = either(below, edge)
 
     @pl.loop(0, heads)
     def _(j):
         for copy in load_kv(j):
             copy.wait()
 
-    pl.semaphore_wait(barrier, jnp.where(edge, 6, 5))
+    pl.semaphore_wait(
+        barrier,
+        3 + jnp.where(edge, 1, 0) + jnp.where(up_open, 1, 0) + jnp.where(down_open, 1, 0),
+    )
 
     @pl.loop(0, heads)
     def _(j):
-        @pl.when(sends_up)
+        @pl.when(sends_up(j))
         def _():
             send_up(j).start()
 
@@ -234,82 +282,162 @@
         at = pl.ds(pl.multiple_of(h * HEAD_DIM, HEAD_DIM), HEAD_DIM)
         return pltpu.make_async_copy(out.at[h], out_hbm.at[:, at], out_sem.at[h])
 
-    shift = jnp.where(edge, 0, half)
-
-    def pass_on(j):
-        @pl.when(relays)
+    def pass_relay(j):
+        @pl.when(has_relay(j))
         def _():
             arrived(RELAY, j)
             send_left(j).start()
 
-            @pl.when(last)
-            def _():
-                send_right(j).start()
-
-            @pl.when(c == 1)
-            def _():
-                send_extra(j).start()
-
-        arrived(BACK1 + c, j)
-        send_side(SIDE1, j, BACK1).start()
-        arrived(BACK3 + c, j)
-        send_side(SIDE3, j, BACK3).start()
-
-        @pl.when(j >= half)
-        def _():
-            send_next(j - shift).start()
-            send_prev(j - shift).start()
+        @pl.when(both(last, below))
+        def _():
+            send_right(j).start()
+
+        @pl.when(relays_extra)
+        def _():
+            send_extra(j).start()
+
+    def pass_aside(j):
+        @pl.when(has1)
+        def _():
+            arrived(BACK1 + c, j)
+            send_side(SIDE1, j, BACK1).start()
+
+        @pl.when(has3)
+        def _():
+            arrived(BACK3 + c, j)
+            send_side(SIDE3, j, BACK3).start()
+
+        @pl.when(passes3(j))
+        def _():
+            arrived(BACK3 + c, j)
+
+    def next_range(step):
+        low = jnp.where(last, 0, 2 * (step - (heads - 2)))
+        high = jnp.where(last, from_left, jnp.minimum(low + 2, from_left))
+        return both(sends_next, step >= jnp.where(last, heads, heads - 2), step <= heads), low, high
+
+    def prev_range(step):
+        low = jnp.where(step == heads, from_right, heads - 1)
+        high = jnp.where(step == heads, heads - 1, heads)
+        return both(sends_prev, step >= heads, step <= heads + 1), low, high
 
     def early_ready(j):
-        arrived(EXTRA, j)
-        arrived(BACK1 + other, j)
-        arrived(BACK3 + other, j)
-
-    @pl.loop(0, heads + 1)
+        @pl.when(has_extra())
+        def _():
+            arrived(EXTRA, j)
+
+        @pl.when(has1)
+        def _():
+            arrived(BACK1 + other, j)
+
+        @pl.when(has3)
+        def _():
+            arrived(BACK3 + other, j)
+
+    @pl.loop(0, heads + 3)
     def _(step):
         @pl.when(step < heads)
         def _():
-            pass_on(step)
-
-        @pl.when(step > 0)
-        def _():
-            early_ready(step - 1)
-            fold_early(step - 1)
-
-    @pl.loop(0, half)
-    def _(step):
-        for j in (step, step + half):
+            pass_relay(step)
+
+        @pl.when(both(step >= 2, step < heads + 2))
+        def _():
+            pass_aside(step - 2)
+
+        sending, low, high = next_range(step)
+
+        @pl.when(sending)
+        def _():
+            @pl.loop(low, high)
+            def _(j):
+                send_next(j).start()
+
+        sending, low, high = prev_range(step)
+
+        @pl.when(sending)
+        def _():
+            @pl.loop(low, high)
+            def _(j):
+                send_prev(j).start()
+
+        @pl.when(step >= 3)
+        def _():
+            early_ready(step - 3)
+            fold_early(step - 3)
+
+    def late_head(k):
+        odd = lax.rem(k, 2)
+        evenly = half * odd + lax.div(k, 2)
+        left_first = jnp.where(
+            odd == 1, lax.div(k + 1, 2), jnp.where(k == 0, 0, half + lax.div(k, 2))
+        )
+        return jnp.where(first, evenly, left_first)
+
+    def pass_late(k):
+        @pl.when(has2)
+        def _():
+            j = late_head(k)
             arrived(BACK2 + c, j)
             send_side(SIDE2, j, BACK2).start()
-        for j in (step, step + half):
+
+    pass_late(0)
+
+    @pl.loop(0, heads)
+    def _(k):
+        @pl.when(k + 1 < heads)
+        def _():
+            pass_late(k + 1)
+
+        j = late_head(k)
+
+        @pl.when(has2)
+        def _():
             arrived(BACK2 + other, j)
-            fold_late(j)
-            for r in range(GROUP):
-                store_out(j * GROUP + r).start()
+
+        fold_late(j)
+        for r in range(GROUP):
+            store_out(j * GROUP + r).start()
 
     @pl.loop(0, heads)
     def _(j):
         for r in range(GROUP):
             store_out(j * GROUP + r).wait()
 
-        @pl.when(sends_up)
+        @pl.when(sends_up(j))
         def _():
             send_up(j).wait_send()
 
-        send_right(j).wait_send()
-        send_left(j).wait_send()
-        send_side(SIDE1, j, BACK1).wait_send()
-        send_side(SIDE2, j, BACK2).wait_send()
-        send_side(SIDE3, j, BACK3).wait_send()
-
-        @pl.when(sends_extra)
+        @pl.when(either(jnp.logical_not(last), below))
+        def _():
+            send_right(j).wait_send()
+
+        @pl.when(either(first, has_relay(j)))
+        def _():
+            send_left(j).wait_send()
+
+        @pl.when(has1)
+        def _():
+            send_side(SIDE1, j, BACK1).wait_send()
+
+        @pl.when(has2)
+        def _():
+            send_side(SIDE2, j, BACK2).wait_send()
+
+        @pl.when(has3)
+        def _():
+            send_side(SIDE3, j, BACK3).wait_send()
+
+        @pl.when(either(c == 0, relays_extra))
         def _():
             send_extra(j).wait_send()
 
-        @pl.when(j >= half)
-        def _():
-            send_next(j - shift).wait_send()
-            send_prev(j - shift).wait_send()
+        @pl.when(both(sends_next, j < from_left))
+        def _():
+            send_next(j).wait_send()
+
+        @pl.when(both(sends_prev, j >= from_right))
+        def _():
+            send_prev(j).wait_send()
 
 
 def shards(sections, queries, keys, values, doc_ids):
@@ -318,7 +446,7 @@
     return pl.pallas_call(
         functools.partial(attention_kernel, sections, rows, heads),
         out_shape=jax.ShapeDtypeStruct(queries.shape, jnp.bfloat16),
-        in_specs=[pl.BlockSpec(memory_space=pl.ANY)] * 4,
+        in_specs=[pl.BlockSpec(memory_space=pltpu.HBM)] * 4,
         out_specs=pl.BlockSpec(memory_space=pl.ANY),
         scratch_shapes=[
             pltpu.VMEM((BLOCKS, heads, 2, rows, HEAD_DIM), jnp.bfloat16),
@@ -337,7 +465,7 @@
             pltpu.SemaphoreType.DMA((heads * GROUP,)),
         ],
         compiler_params=pltpu.CompilerParams(
-            collective_id=0, has_side_effects=True, vmem_limit_bytes=60 * 1024 * 1024
+            collective_id=0, has_side_effects=True, vmem_limit_bytes=40 * 1024 * 1024
         ),
     )(queries, keys, values, docs)
 

time: 79.8 us -> 67.4 us (0.84)
  the two profiles are of different devices: /device:TPU:8 before, /device:TPU:185 now
where the time goes in v1:
time: 67.4 us; the launch traced here: 67.1 us
  Pallas kernels  61.5 us (91%)
  local copies, waits for them, and re-layouts  5.58 us (8%)
    pallas_call x1, Pallas kernels, shards(): pl.pallas_call(functools.partial(attention_kernel, sections, rows, heads)...  61.5 us
    unnamed x9, local copies, waits for them, and re-layouts  5.58 us

profile of v1, /device:TPU:185, one launch (start us, length us, event | category | flops | bytes accessed | tf_op | source)
XLA Modules:
  0.0 67.1 jit_solution(11630806278363718966)
XLA Ops:
  0.0 0.0 copy-start
  0.0 1.4 %copy-done = bf16[256,3072]{1,0:T(8,128)(2,1)S(1)} copy-done((bf16[256,3072]{1,0:T(8,128)(2,1)S(1)}, bf16[256,3072]{1,0:T(8,128)(2,1)}, u32[]{:S(2)}) %copy-start) | copy-done | bytes 1572888
  1.4 0.0 copy-start.1
  1.4 1.0 %copy-done.1 = bf16[256,1024]{1,0:T(8,128)(2,1)S(1)} copy-done((bf16[256,1024]{1,0:T(8,128)(2,1)S(1)}, bf16[256,1024]{1,0:T(8,128)(2,1)}, u32[]{:S(2)}) %copy-start.1) | copy-done | bytes 524312
  2.5 0.0 copy-start.2
  2.5 1.0 %copy-done.2 = bf16[256,1024]{1,0:T(8,128)(2,1)S(1)} copy-done((bf16[256,1024]{1,0:T(8,128)(2,1)S(1)}, bf16[256,1024]{1,0:T(8,128)(2,1)}, u32[]{:S(2)}) %copy-start.2) | copy-done | bytes 524312
  3.5 0.0 copy-start.3
  3.5 0.9 %copy-done.3 = s32[65536]{0:T(1024)S(1)} copy-done((s32[65536]{0:T(1024)S(1)}, s32[65536]{0:T(1024)}, u32[]{:S(2)}) %copy-start.3) | copy-done | bytes 262168
  4.4 61.5 %shard_map.46 = bf16[256,3072]{1,0:T(8,128)(2,1)S(1)} custom-call(bf16[256,3072]{1,0:T(8,128)(2,1)S(1)} %copy-done, bf16[256,1024]{1,0:T(8,128)(2,1)S(1)} %copy-done.1, bf16[256,1024]{1,0:T(8,128)(2,1)S(1)} %copy-done.2, s32[512,128]{1,0:T(8,128)S(1)} %bitcast.1), custom_call_target="tpu_custom_call" | custom-call | tf_op jit(solution)/shard_map/pallas_call | solution.py:446
  66.0 1.1 %copy.6 = bf16[256,3072]{1,0:T(8,128)(2,1)} copy(bf16[256,3072]{1,0:T(8,128)(2,1)S(1)} %shard_map.46) | data formatting | bytes 3145728
Async XLA Ops:
  0.0 1.4 %copy-start = (bf16[256,3072]{1,0:T(8,128)(2,1)S(1)}, bf16[256,3072]{1,0:T(8,128)(2,1)}, u32[]{:S(2)}) copy-start(bf16[256,3072]{1,0:T(8,128)(2,1)} %q_hbm.1) | copy-start | bytes 4718596
  1.4 1.0 %copy-start.1 = (bf16[256,1024]{1,0:T(8,128)(2,1)S(1)}, bf16[256,1024]{1,0:T(8,128)(2,1)}, u32[]{:S(2)}) copy-start(bf16[256,1024]{1,0:T(8,128)(2,1)} %k_hbm.1) | copy-start | bytes 1572868
  2.5 1.0 %copy-start.2 = (bf16[256,1024]{1,0:T(8,128)(2,1)S(1)}, bf16[256,1024]{1,0:T(8,128)(2,1)}, u32[]{:S(2)}) copy-start(bf16[256,1024]{1,0:T(8,128)(2,1)} %v_hbm.1) | copy-start | bytes 1572868
  3.5 0.9 %copy-start.3 = (s32[65536]{0:T(1024)S(1)}, s32[65536]{0:T(1024)}, u32[]{:S(2)}) copy-start(s32[65536]{0:T(1024)} %param.7) | copy-start | bytes 786436

commit v2 on v1

--- a/solution.py
+++ b/solution.py
@@ -15,10 +15,10 @@
 LANES = 128
 NEG = -1e30
 
-OWN, EXTRA, BACK1, BACK2, BACK3, RELAY = 0, 1, 2, 4, 6, 8
-BLOCKS = 9
-UP, RIGHT, LEFT, NEXT, PREV, SIDE_EXTRA, SIDE1, SIDE2, SIDE3 = range(9)
-KINDS = 9
+OWN, EXTRA, BACK1, BACK2, BACK3, RELAY, RELAY2 = 0, 1, 2, 4, 6, 8, 9
+BLOCKS = 10
+UP, RIGHT, LEFT, NEXT, PREV, SIDE_EXTRA, SIDE1, SIDE2, SIDE3, ROUND = range(10)
+KINDS = 10
 
 
 def attention_kernel(
@@ -143,7 +143,11 @@
         return send(LEFT, j, left_source, BACK3 + c, left, c)
 
     def send_next(j):
-        return send(NEXT, j, BACK1 + c, BACK2 + c, following, c)
+        target = jnp.where(last, RELAY2, BACK2 + c)
+        return send(NEXT, j, BACK1 + c, target, jnp.where(last, up, following), c)
+
+    def send_round(j):
+        return send(ROUND, j, RELAY2, BACK2 + c, right, c)
 
     def send_prev(j):
         return send(PREV, j, BACK3 + c, BACK2 + c, previous, c)
@@ -220,20 +224,23 @@
         for piece in range(pieces):
             row = (4 + parity - back) * (2 * pieces) + core * pieces + piece
             same = jnp.where(docs[pl.ds(row, 1), :] == ids, 1.0, 0.0)
-            turned = jnp.transpose(same)
-            onehot[block, piece * LANES:(piece + 1) * LANES, :] = turned.astype(jnp.bfloat16)
-            if block == 0:
-                away[piece * LANES:(piece + 1) * LANES, :] = ((1.0 - turned) * NEG).astype(jnp.bfloat16)
+            span = slice(piece * LANES, (piece + 1) * LANES)
+            onehot[block, :, span] = same.astype(jnp.bfloat16)
+            if block == OWN:
+                away[span, :] = jnp.transpose((1.0 - same) * NEG).astype(jnp.bfloat16)
 
     @pl.loop(0, heads * GROUP)
     def _(h):
         load_q(h).wait()
 
-    def scores(query, block, j):
-        key = jnp.concatenate([kv[block, j, 0], onehot[block]], axis=1)
-        return lax.dot_general(
-            query, key, (((1,), (1,)), ((), ())), preferred_element_type=jnp.float32
-        )
+    def keys_of(block, j):
+        return jnp.concatenate([jnp.transpose(kv[block, j, 0]), onehot[block]], axis=0)
+
+    def scores(query, key):
+        return jnp.dot(query, key, preferred_element_type=jnp.float32)
+
+    def wide(column):
+        return jnp.concatenate([column] * (rows // LANES), axis=1)
 
     def values_of(block, j):
         value = kv[block, j, 1]
@@ -252,31 +259,40 @@
 
     early = (OWN, EXTRA, BACK1, BACK1 + 1, BACK3, BACK3 + 1)
     late = (BACK2, BACK2 + 1)
+    causal = lax.broadcasted_iota(jnp.int32, (rows, rows), 1) <= lax.broadcasted_iota(
+        jnp.int32, (rows, rows), 0
+    )
+
+    def row_max(parts):
+        return jnp.broadcast_to(
+            jnp.max(functools.reduce(jnp.maximum, parts), axis=1, keepdims=True), (rows, LANES)
+        )
+
+    def finish_late(j, r, parts):
+        old = stat_max[j, r]
+        top = jnp.maximum(old, row_max(parts))
+        rescale = jnp.exp2((old - top) * scale)
+        summed = acc[j, r] * wide(rescale) + weigh(parts, wide(top), late, j)
+        out[j * GROUP + r] = (summed[:, :HEAD_DIM] / summed[:, HEAD_DIM:]).astype(jnp.bfloat16)
+
+    def finish_early(j, r, parts):
+        parts[0] = jnp.where(causal, parts[0], NEG)
+        top = row_max(parts)
+        stat_max[j, r] = top
+        acc[j, r] = weigh(parts, wide(top), early, j)
+
+    def all_scores(blocks, j):
+        query = jnp.concatenate([query_of(j, r) for r in range(GROUP)], axis=0)
+        whole = [scores(query, key) for key in [keys_of(block, j) for block in blocks]]
+        return [[part[r * rows:(r + 1) * rows] for part in whole] for r in range(GROUP)]
 
     def fold_early(j):
-        causal = lax.broadcasted_iota(jnp.int32, (rows, rows), 1) <= lax.broadcasted_iota(
-            jnp.int32, (rows, rows), 0
-        )
-        for r in range(GROUP):
-            query = query_of(j, r)
-            parts = [scores(query, block, j) for block in early]
-            parts[0] = jnp.where(causal, parts[0], NEG)
-            highest = functools.reduce(jnp.maximum, parts)
-            top = jnp.max(highest, axis=1, keepdims=True)
-            stat_max[j, r] = jnp.broadcast_to(top, (rows, LANES))
-            acc[j, r] = weigh(parts, top, early, j)
+        for r, parts in enumerate(all_scores(early, j)):
+            finish_early(j, r, parts)
 
     def fold_late(j):
-        for r in range(GROUP):
-            query = query_of(j, r)
-            parts = [scores(query, block, j) for block in late]
-            old = stat_max[j, r]
-            highest = functools.reduce(jnp.maximum, parts)
-            top = jnp.maximum(old[:, :1], jnp.max(highest, axis=1, keepdims=True))
-            rescale = jnp.exp2((old[:, :1] - top) * scale)
-            summed = acc[j, r] * rescale + weigh(parts, top, late, j)
-            result = summed[:, :HEAD_DIM] / summed[:, HEAD_DIM:]
-            out[j * GROUP + r] = result.astype(jnp.bfloat16)
+        for r, parts in enumerate(all_scores(late, j)):
+            finish_late(j, r, parts)
 
     def store_out(h):
         at = pl.ds(pl.multiple_of(h * HEAD_DIM, HEAD_DIM), HEAD_DIM)
@@ -312,9 +328,15 @@
             arrived(BACK3 + c, j)
 
     def next_range(step):
-        low = jnp.where(last, 0, 2 * (step - (heads - 2)))
-        high = jnp.where(last, from_left, jnp.minimum(low + 2, from_left))
-        return both(sends_next, step >= jnp.where(last, heads, heads - 2), step <= heads), low, high
+        low = 2 * (step - (heads - 2))
+        high = jnp.minimum(low + 2, from_left)
+        return both(sends_next, step >= heads - 2, step <= heads), low, high
+
+    rounds = both(last, below)
+
+    def pass_round(j):
+        arrived(RELAY2, j)
+        send_round(j).start()
 
     def prev_range(step):
         low = jnp.where(step == heads, from_right, heads - 1)
@@ -359,6 +381,10 @@
             @pl.loop(low, high)
             def _(j):
                 send_prev(j).start()
+
+        @pl.when(both(rounds, step > heads))
+        def _():
+            pass_round(step - (heads + 1))
 
         @pl.when(step >= 3)
         def _():
@@ -384,6 +410,10 @@
 
     @pl.loop(0, heads)
     def _(k):
+        @pl.when(both(rounds, either(k == 0, k == 2)))
+        def _():
+            pass_round(2 + lax.div(k, 2))
+
         @pl.when(k + 1 < heads)
         def _():
             pass_late(k + 1)
@@ -434,6 +464,10 @@
         @pl.when(both(sends_next, j < from_left))
         def _():
             send_next(j).wait_send()
+
+        @pl.when(both(rounds, j < half))
+        def _():
+            send_round(j).wait_send()
 
         @pl.when(both(sends_prev, j >= from_right))
         def _():
@@ -451,7 +485,7 @@
         scratch_shapes=[
             pltpu.VMEM((BLOCKS, heads, 2, rows, HEAD_DIM), jnp.bfloat16),
             pltpu.VMEM((heads * GROUP, rows, HEAD_DIM), jnp.bfloat16),
-            pltpu.VMEM((RELAY, rows, LANES), jnp.bfloat16),
+            pltpu.VMEM((RELAY, LANES, rows), jnp.bfloat16),
             pltpu.VMEM((rows, LANES), jnp.bfloat16),
             pltpu.VMEM((24, LANES), jnp.int32),
             pltpu.VMEM((heads, GROUP, rows, LANES), jnp.float32),
@@ -467,7 +501,7 @@
         compiler_params=pltpu.CompilerParams(
             collective_id=0, has_side_effects=True, vmem_limit_bytes=40 * 1024 * 1024
         ),
-    )(queries, keys, values, docs)
+    )(*[pltpu.with_memory_space_constraint(a, pltpu.HBM) for a in (queries, keys, values, docs)])
 
 
 def solution(mesh):

time: 67.4 us -> 59.8 us (0.89)
  the two profiles are of different devices: /device:TPU:185 before, /device:TPU:7 now
where the time goes in v2:
time: 59.8 us; the launch traced here: 59.6 us
  Pallas kernels  58.4 us (98%)
  local copies, waits for them, and re-layouts  1.15 us (2%)
    pallas_call x1, Pallas kernels, shards(): pl.pallas_call(functools.partial(attention_kernel, sections, rows, heads)...  58.4 us

profile of v2, /device:TPU:7, one launch (start us, length us, event | category | flops | bytes accessed | tf_op | source)
XLA Modules:
  0.0 59.6 jit_solution(14828169664677342257)
XLA Ops:
  0.0 58.4 %shard_map.46 = bf16[256,3072]{1,0:T(8,128)(2,1)S(1)} custom-call(bf16[256,3072]{1,0:T(8,128)(2,1)} %q_hbm.1, bf16[256,1024]{1,0:T(8,128)(2,1)} %k_hbm.1, bf16[256,1024]{1,0:T(8,128)(2,1)} %v_hbm.1, s32[512,128]{1,0:T(8,128)} %bitcast.1), custom_call_target="tpu_custom_call" | custom-call | tf_op jit(solution)/shard_map/pallas_call | solution.py:480
  58.4 1.1 %copy.6 = bf16[256,3072]{1,0:T(8,128)(2,1)} copy(bf16[256,3072]{1,0:T(8,128)(2,1)S(1)} %shard_map.46) | data formatting | bytes 3145728

commit v3 on v2

--- a/solution.py
+++ b/solution.py
@@ -34,12 +34,11 @@
     x = lax.rem(s, RING)
     row_start = s - x
     first, last = x == 0, x == RING - 1
-    edge = jnp.logical_or(first, last)
     top, bottom = s < RING, s >= sections - RING
     below = jnp.logical_not(top)
-    from_left = jnp.where(last, half, half + 1)
+    from_left = jnp.where(last, half, jnp.where(jnp.logical_and(bottom, x == 2), heads, half + 1))
     from_right = jnp.where(x == 1, half, half + 1)
-    wrapped = half + 1
+    turned_from = half + 1
 
     right = row_start + lax.rem(x + 1, RING)
     left = row_start + lax.rem(x + RING - 1, RING)
@@ -85,8 +84,8 @@
             def _(j):
                 kv[block, j] = jnp.zeros((2, rows, HEAD_DIM), kv.dtype)
 
-    up_open = jnp.logical_or(s < sections - RING, x == 1)
-    down_open = jnp.logical_or(s >= RING, x == 1)
+    up_open = jnp.logical_not(bottom)
+    down_open = below
 
     barrier = pltpu.get_barrier_semaphore()
 
@@ -104,11 +103,14 @@
     def _():
         greet(down, up_core)
 
-    @pl.when(first)
+    from_next = jnp.logical_and(last, up_open)
+    to_previous = jnp.logical_and(first, down_open)
+
+    @pl.when(to_previous)
     def _():
         greet(previous, c)
 
-    @pl.when(last)
+    @pl.when(from_next)
     def _():
         greet(following, c)
 
@@ -131,7 +133,8 @@
 
     up_target = jnp.where(first, EXTRA, RELAY)
     right_source = jnp.where(last, RELAY, OWN)
-    left_source = jnp.where(first, OWN, RELAY)
+    left_source = jnp.where(jnp.logical_or(first, top), OWN, RELAY)
+    left_target = jnp.where(jnp.logical_and(top, x == 1), RELAY2, BACK3 + c)
 
     def send_up(j):
         return send(UP, j, OWN, up_target, up, up_core)
@@ -140,14 +143,14 @@
         return send(RIGHT, j, right_source, BACK1 + c, right, c)
 
     def send_left(j):
-        return send(LEFT, j, left_source, BACK3 + c, left, c)
+        return send(LEFT, j, left_source, left_target, left, c)
 
     def send_next(j):
         target = jnp.where(last, RELAY2, BACK2 + c)
         return send(NEXT, j, BACK1 + c, target, jnp.where(last, up, following), c)
 
     def send_round(j):
-        return send(ROUND, j, RELAY2, BACK2 + c, right, c)
+        return send(ROUND, j, RELAY2, BACK2 + c, jnp.where(first, left, right), c)
 
     def send_prev(j):
         return send(PREV, j, BACK3 + c, BACK2 + c, previous, c)
@@ -164,27 +167,21 @@
     def either(*conditions):
         return functools.reduce(jnp.logical_or, conditions)
 
-    inside = jnp.logical_not(bottom)
-
-    def sends_up(j):
-        return either(both(first, c == 1, inside), both(x > 0, inside), both(x == 1, bottom, j >= wrapped))
-
-    def has_relay(j):
-        return both(x > 0, either(below, both(x == 1, j >= wrapped)))
+    sends_up = both(either(x > 0, c == 1), up_open)
+    has_relay = both(x > 0, below)
+    turns = both(top, x == 1)
+    turns_on = both(top, first)
 
     has1 = either(below, x > 0)
     has2 = either(below, x > 1)
     has3 = either(below, last)
 
-    def passes3(j):
-        return both(first, top, j >= wrapped)
-
     def has_extra():
         return either(c == 1, below)
 
     relays_extra = both(x > 0, below, c == 1)
     sends_next = both(has1, jnp.logical_not(both(bottom, last)))
-    sends_prev = either(below, edge)
+    sends_prev = either(both(below, s != RING), last)
 
     @pl.loop(0, heads)
     def _(j):
@@ -193,12 +190,12 @@
 
     pl.semaphore_wait(
         barrier,
-        3 + jnp.where(edge, 1, 0) + jnp.where(up_open, 1, 0) + jnp.where(down_open, 1, 0),
+        3 + jnp.where(jnp.logical_or(from_next, to_previous), 1, 0) + jnp.where(up_open, 1, 0) + jnp.where(down_open, 1, 0),
     )
 
     @pl.loop(0, heads)
     def _(j):
-        @pl.when(sends_up(j))
+        @pl.when(sends_up)
         def _():
             send_up(j).start()
 
@@ -206,7 +203,7 @@
         def _():
             send_right(j).start()
 
-        @pl.when(first)
+        @pl.when(either(first, both(turns, j >= turned_from)))
         def _():
             send_left(j).start()
 
@@ -299,7 +296,7 @@
         return pltpu.make_async_copy(out.at[h], out_hbm.at[:, at], out_sem.at[h])
 
     def pass_relay(j):
-        @pl.when(has_relay(j))
+        @pl.when(has_relay)
         def _():
             arrived(RELAY, j)
             send_left(j).start()
@@ -322,15 +319,11 @@
         def _():
             arrived(BACK3 + c, j)
             send_side(SIDE3, j, BACK3).start()
-
-        @pl.when(passes3(j))
-        def _():
-            arrived(BACK3 + c, j)
 
     def next_range(step):
         low = 2 * (step - (heads - 2))
         high = jnp.minimum(low + 2, from_left)
-        return both(sends_next, step >= heads - 2, step <= heads), low, high
+        return both(sends_next, step >= heads - 2, step <= heads + 1), low, high
 
     rounds = both(last, below)
 
@@ -381,6 +374,10 @@
             @pl.loop(low, high)
             def _(j):
                 send_prev(j).start()
+
+        @pl.when(both(turns_on, step >= turned_from, step < heads))
+        def _():
+            pass_round(step)
 
         @pl.when(both(rounds, step > heads))
         def _():
@@ -433,7 +430,7 @@
         for r in range(GROUP):
             store_out(j * GROUP + r).wait()
 
-        @pl.when(sends_up(j))
+        @pl.when(sends_up)
         def _():
             send_up(j).wait_send()
 
@@ -441,7 +438,7 @@
         def _():
             send_right(j).wait_send()
 
-        @pl.when(either(first, has_relay(j)))
+        @pl.when(either(first, has_relay, both(turns, j >= turned_from)))
         def _():
             send_left(j).wait_send()
 
@@ -465,7 +462,7 @@
         def _():
             send_next(j).wait_send()
 
-        @pl.when(both(rounds, j < half))
+        @pl.when(either(both(rounds, j < half), both(turns_on, j >= turned_from)))
         def _():
             send_round(j).wait_send()
 

time: 59.8 us -> 56.9 us (0.952)
  the two profiles are of different devices: /device:TPU:7 before, /device:TPU:249 now
where the time goes in v3:
time: 56.9 us; the launch traced here: 56.7 us
  Pallas kernels  55.6 us (98%)
  local copies, waits for them, and re-layouts  1.15 us (2%)
    pallas_call x1, Pallas kernels, shards(): pl.pallas_call(functools.partial(attention_kernel, sections, rows, heads)...  55.6 us
    unnamed x1, local copies, waits for them, and re-layouts  1.15 us

profile of v3, /device:TPU:249, one launch (start us, length us, event | category | flops | bytes accessed | tf_op | source)
XLA Modules:
  0.0 56.7 jit_solution(3057230483495991850)
XLA Ops:
  0.0 55.6 %shard_map.46 = bf16[256,3072]{1,0:T(8,128)(2,1)S(1)} custom-call(bf16[256,3072]{1,0:T(8,128)(2,1)} %q_hbm.1, bf16[256,1024]{1,0:T(8,128)(2,1)} %k_hbm.1, bf16[256,1024]{1,0:T(8,128)(2,1)} %v_hbm.1, s32[512,128]{1,0:T(8,128)} %bitcast.1), custom_call_target="tpu_custom_call" | custom-call | tf_op jit(solution)/shard_map/pallas_call | solution.py:477
  55.6 1.1 %copy.6 = bf16[256,3072]{1,0:T(8,128)(2,1)} copy(bf16[256,3072]{1,0:T(8,128)(2,1)S(1)} %shard_map.46) | data formatting | bytes 3145728

commit v4 on v3

--- a/solution.py
+++ b/solution.py
@@ -17,8 +17,8 @@
 
 OWN, EXTRA, BACK1, BACK2, BACK3, RELAY, RELAY2 = 0, 1, 2, 4, 6, 8, 9
 BLOCKS = 10
-UP, RIGHT, LEFT, NEXT, PREV, SIDE_EXTRA, SIDE1, SIDE2, SIDE3, ROUND = range(10)
-KINDS = 10
+UP, RIGHT, LEFT, NEXT, PREV, SIDE_EXTRA, SIDE1, SIDE2, SIDE3, ROUND, CROSS1, CROSS3 = range(12)
+KINDS = 12
 
 
 def attention_kernel(
@@ -36,9 +36,8 @@
     first, last = x == 0, x == RING - 1
     top, bottom = s < RING, s >= sections - RING
     below = jnp.logical_not(top)
-    from_left = jnp.where(last, half, jnp.where(jnp.logical_and(bottom, x == 2), heads, half + 1))
-    from_right = jnp.where(x == 1, half, half + 1)
-    turned_from = half + 1
+    from_left = jnp.where(jnp.logical_and(bottom, x == 2), heads, half)
+    express = heads - 2
 
     right = row_start + lax.rem(x + 1, RING)
     left = row_start + lax.rem(x + RING - 1, RING)
@@ -109,6 +108,11 @@
     @pl.when(to_previous)
     def _():
         greet(previous, c)
+        greet(down, c)
+
+    @pl.when(jnp.logical_and(first, up_open))
+    def _():
+        greet(up, c)
 
     @pl.when(from_next)
     def _():
@@ -132,18 +136,25 @@
         send(UP, j, block, block, s, other).wait_recv()
 
     up_target = jnp.where(first, EXTRA, RELAY)
-    right_source = jnp.where(last, RELAY, OWN)
-    left_source = jnp.where(jnp.logical_or(first, top), OWN, RELAY)
-    left_target = jnp.where(jnp.logical_and(top, x == 1), RELAY2, BACK3 + c)
-
     def send_up(j):
         return send(UP, j, OWN, up_target, up, up_core)
 
     def send_right(j):
-        return send(RIGHT, j, right_source, BACK1 + c, right, c)
+        ahead = jnp.logical_and(last, j >= express)
+        source = jnp.where(jnp.logical_and(last, j < express), RELAY, OWN)
+        return send(RIGHT, j, source, jnp.where(ahead, RELAY, BACK1 + c), right, c)
 
     def send_left(j):
-        return send(LEFT, j, left_source, left_target, left, c)
+        own = jnp.logical_or(jnp.logical_or(first, top), j >= express)
+        ahead = jnp.logical_and(own, x > 0)
+        source = jnp.where(own, OWN, RELAY)
+        return send(LEFT, j, source, jnp.where(ahead, RELAY2, BACK3 + c), left, c)
+
+    def send_cross1(j):
+        return send(CROSS1, j, RELAY, BACK1 + c, up, c)
+
+    def send_cross3(j):
+        return send(CROSS3, j, RELAY2, BACK3 + c, up, c)
 
     def send_next(j):
         target = jnp.where(last, RELAY2, BACK2 + c)
@@ -167,8 +178,20 @@
     def either(*conditions):
         return functools.reduce(jnp.logical_or, conditions)
 
-    sends_up = both(either(x > 0, c == 1), up_open)
-    has_relay = both(x > 0, below)
+    def sends_up(j):
+        return both(up_open, either(c == 1, both(x > 0, j < express)))
+
+    def right_ahead(j):
+        return either(jnp.logical_not(last), both(up_open, j >= express))
+
+    def left_ahead(j):
+        return either(first, both(x > 0, up_open, j >= express), both(turns, j >= half))
+
+    def relays(j):
+        return both(x > 0, below, j < express)
+
+    crosses1 = both(first, up_open)
+    crosses3 = both(jnp.logical_not(last), up_open)
     turns = both(top, x == 1)
     turns_on = both(top, first)
 
@@ -190,20 +213,24 @@
 
     pl.semaphore_wait(
         barrier,
-        3 + jnp.where(jnp.logical_or(from_next, to_previous), 1, 0) + jnp.where(up_open, 1, 0) + jnp.where(down_open, 1, 0),
+        3
+        + jnp.where(from_next, 1, 0)
+        + jnp.where(to_previous, 2, 0)
+        + jnp.where(jnp.logical_and(first, up_open), 1, 0)
+        + jnp.where(up_open, 1, 0) + jnp.where(down_open, 1, 0),
     )
 
     @pl.loop(0, heads)
     def _(j):
-        @pl.when(sends_up)
+        @pl.when(sends_up(j))
         def _():
             send_up(j).start()
 
-        @pl.when(jnp.logical_not(last))
+        @pl.when(right_ahead(j))
         def _():
             send_right(j).start()
 
-        @pl.when(either(first, both(turns, j >= turned_from)))
+        @pl.when(left_ahead(j))
         def _():
             send_left(j).start()
 
@@ -296,18 +323,33 @@
         return pltpu.make_async_copy(out.at[h], out_hbm.at[:, at], out_sem.at[h])
 
     def pass_relay(j):
-        @pl.when(has_relay)
+        @pl.when(relays(j))
         def _():
             arrived(RELAY, j)
             send_left(j).start()
 
-        @pl.when(both(last, below))
+        @pl.when(both(relays_extra, j >= express))
+        def _():
+            arrived(RELAY, j)
+
+        @pl.when(both(last, relays(j)))
         def _():
             send_right(j).start()
 
         @pl.when(relays_extra)
         def _():
             send_extra(j).start()
+
+    def pass_across(j):
+        @pl.when(crosses3)
+        def _():
+            arrived(RELAY2, j)
+            send_cross3(j).start()
+
+        @pl.when(crosses1)
+        def _():
+            arrived(RELAY, j)
+            send_cross1(j).start()
 
     def pass_aside(j):
         @pl.when(has1)
@@ -321,20 +363,19 @@
             send_side(SIDE3, j, BACK3).start()
 
     def next_range(step):
-        low = 2 * (step - (heads - 2))
-        high = jnp.minimum(low + 2, from_left)
-        return both(sends_next, step >= heads - 2, step <= heads + 1), low, high
+        in_pairs = step < heads
+        low = jnp.where(in_pairs, 2 * (step - (heads - 3)), step - 2)
+        high = jnp.minimum(low + jnp.where(in_pairs, 2, 1), from_left)
+        return both(sends_next, step >= heads - 3, step <= heads + 1), low, high
 
     rounds = both(last, below)
 
     def pass_round(j):
-        arrived(RELAY2, j)
+        @pl.when(j < express)
+        def _():
+            arrived(RELAY2, j)
+
         send_round(j).start()
-
-    def prev_range(step):
-        low = jnp.where(step == heads, from_right, heads - 1)
-        high = jnp.where(step == heads, heads - 1, heads)
-        return both(sends_prev, step >= heads, step <= heads + 1), low, high
 
     def early_ready(j):
         @pl.when(has_extra())
@@ -367,21 +408,22 @@
             def _(j):
                 send_next(j).start()
 
-        sending, low, high = prev_range(step)
-
-        @pl.when(sending)
-        def _():
-            @pl.loop(low, high)
-            def _(j):
-                send_prev(j).start()
-
-        @pl.when(both(turns_on, step >= turned_from, step < heads))
+        @pl.when(both(sends_prev, step >= half + 2, step < heads + 2))
+        def _():
+            send_prev(step - 2).start()
+
+        @pl.when(step == 2)
+        def _():
+            for j in range(express, heads):
+                pass_across(j)
+
+        @pl.when(both(turns_on, step >= half, step < heads))
         def _():
             pass_round(step)
 
-        @pl.when(both(rounds, step > heads))
-        def _():
-            pass_round(step - (heads + 1))
+        @pl.when(both(rounds, step >= heads))
+        def _():
+            pass_round(step - heads)
 
         @pl.when(step >= 3)
         def _():
@@ -391,10 +433,7 @@
     def late_head(k):
         odd = lax.rem(k, 2)
         evenly = half * odd + lax.div(k, 2)
-        left_first = jnp.where(
-            odd == 1, lax.div(k + 1, 2), jnp.where(k == 0, 0, half + lax.div(k, 2))
-        )
-        return jnp.where(first, evenly, left_first)
+        return jnp.where(both(bottom, last), k, evenly)
 
     def pass_late(k):
         @pl.when(has2)
@@ -407,9 +446,9 @@
 
     @pl.loop(0, heads)
     def _(k):
-        @pl.when(both(rounds, either(k == 0, k == 2)))
-        def _():
-            pass_round(2 + lax.div(k, 2))
+        @pl.when(both(rounds, k == 1))
+        def _():
+            pass_round(half - 1)
 
         @pl.when(k + 1 < heads)
         def _():
@@ -430,15 +469,23 @@
         for r in range(GROUP):
             store_out(j * GROUP + r).wait()
 
-        @pl.when(sends_up)
+        @pl.when(sends_up(j))
         def _():
             send_up(j).wait_send()
 
-        @pl.when(either(jnp.logical_not(last), below))
+        @pl.when(either(right_ahead(j), both(below, j < express)))
         def _():
             send_right(j).wait_send()
 
-        @pl.when(either(first, has_relay, both(turns, j >= turned_from)))
+        @pl.when(both(crosses1, j >= express))
+        def _():
+            send_cross1(j).wait_send()
+
+        @pl.when(both(crosses3, j >= express))
+        def _():
+            send_cross3(j).wait_send()
+
+        @pl.when(either(left_ahead(j), relays(j)))
         def _():
             send_left(j).wait_send()
 
@@ -462,11 +509,11 @@
         def _():
             send_next(j).wait_send()
 
-        @pl.when(either(both(rounds, j < half), both(turns_on, j >= turned_from)))
+        @pl.when(either(both(rounds, j < half), both(turns_on, j >= half)))
         def _():
             send_round(j).wait_send()
 
-        @pl.when(both(sends_prev, j >= from_right))
+        @pl.when(both(sends_prev, j >= half))
         def _():
             send_prev(j).wait_send()
 

time: 56.9 us -> 59.6 us (1.047)
  the two profiles are of different devices: /device:TPU:249 before, /device:TPU:193 now
where the time goes in v4:
time: 59.6 us; the launch traced here: 59.4 us
  Pallas kernels  58.2 us (98%)
  local copies, waits for them, and re-layouts  1.15 us (2%)
    pallas_call x1, Pallas kernels, shards(): pl.pallas_call(functools.partial(attention_kernel, sections, rows, heads)...  58.2 us

profile of v4, /device:TPU:193, one launch (start us, length us, event | category | flops | bytes accessed | tf_op | source)
XLA Modules:
  0.0 59.4 jit_solution(2181379593590224846)
XLA Ops:
  0.0 58.2 %shard_map.46 = bf16[256,3072]{1,0:T(8,128)(2,1)S(1)} custom-call(bf16[256,3072]{1,0:T(8,128)(2,1)} %q_hbm.1, bf16[256,1024]{1,0:T(8,128)(2,1)} %k_hbm.1, bf16[256,1024]{1,0:T(8,128)(2,1)} %v_hbm.1, s32[512,128]{1,0:T(8,128)} %bitcast.1), custom_call_target="tpu_custom_call" | custom-call | tf_op jit(solution)/shard_map/pallas_call | solution.py:524
  58.3 1.1 %copy.6 = bf16[256,3072]{1,0:T(8,128)(2,1)} copy(bf16[256,3072]{1,0:T(8,128)(2,1)S(1)} %shard_map.46) | data formatting | bytes 3145728

commit v5 on v4

--- a/solution.py
+++ b/solution.py
@@ -17,8 +17,8 @@
 
 OWN, EXTRA, BACK1, BACK2, BACK3, RELAY, RELAY2 = 0, 1, 2, 4, 6, 8, 9
 BLOCKS = 10
-UP, RIGHT, LEFT, NEXT, PREV, SIDE_EXTRA, SIDE1, SIDE2, SIDE3, ROUND, CROSS1, CROSS3 = range(12)
-KINDS = 12
+UP, RIGHT, LEFT, NEXT, PREV, SIDE_EXTRA, SIDE1, SIDE2, SIDE3, ROUND, CROSS1, CROSS3, DOWN = range(13)
+KINDS = 13
 
 
 def attention_kernel(
@@ -36,7 +36,8 @@
     first, last = x == 0, x == RING - 1
     top, bottom = s < RING, s >= sections - RING
     below = jnp.logical_not(top)
-    from_left = jnp.where(jnp.logical_and(bottom, x == 2), heads, half)
+    from_left = jnp.where(jnp.logical_and(bottom, x == 2), heads - 2, half)
+    crossing = jnp.logical_and(lax.rem(s, RING * RING) < RING, below)
     express = heads - 2
 
     right = row_start + lax.rem(x + 1, RING)
@@ -164,7 +165,12 @@
         return send(ROUND, j, RELAY2, BACK2 + c, jnp.where(first, left, right), c)
 
     def send_prev(j):
-        return send(PREV, j, BACK3 + c, BACK2 + c, previous, c)
+        around = jnp.logical_and(first, crossing)
+        target = jnp.where(around, RELAY2, BACK2 + c)
+        return send(PREV, j, BACK3 + c, target, jnp.where(around, left, previous), c)
+
+    def send_down(j):
+        return send(DOWN, j, RELAY2, BACK2 + c, down, c)
 
     def send_extra(j):
         return send(SIDE_EXTRA, j, jnp.where(c == 0, OWN, RELAY), EXTRA, s, other)
@@ -185,15 +191,21 @@
         return either(jnp.logical_not(last), both(up_open, j >= express))
 
     def left_ahead(j):
-        return either(first, both(x > 0, up_open, j >= express), both(turns, j >= half))
+        return either(
+            first,
+            both(x > 0, either(up_open, x == 1), j >= express),
+            both(top, x == 1, j >= half),
+        )
 
     def relays(j):
         return both(x > 0, below, j < express)
 
     crosses1 = both(first, up_open)
     crosses3 = both(jnp.logical_not(last), up_open)
-    turns = both(top, x == 1)
-    turns_on = both(top, first)
+    descends = both(last, crossing)
+
+    def turns_on(j):
+        return both(first, either(both(top, j >= half), both(bottom, j >= express)))
 
     has1 = either(below, x > 0)
     has2 = either(below, x > 1)
@@ -371,11 +383,15 @@
     rounds = both(last, below)
 
     def pass_round(j):
-        @pl.when(j < express)
+        @pl.when(either(j < express, bottom))
         def _():
             arrived(RELAY2, j)
 
         send_round(j).start()
+
+    def pass_down(j):
+        arrived(RELAY2, j)
+        send_down(j).start()
 
     def early_ready(j):
         @pl.when(has_extra())
@@ -417,13 +433,17 @@
             for j in range(express, heads):
                 pass_across(j)
 
-        @pl.when(both(turns_on, step >= half, step < heads))
+        @pl.when(both(turns_on(step), step < heads))
         def _():
             pass_round(step)
 
         @pl.when(both(rounds, step >= heads))
         def _():
             pass_round(step - heads)
+
+        @pl.when(both(descends, step > heads))
+        def _():
+            pass_down(half + step - (heads + 1))
 
         @pl.when(step >= 3)
         def _():
@@ -433,7 +453,8 @@
     def late_head(k):
         odd = lax.rem(k, 2)
         evenly = half * odd + lax.div(k, 2)
-        return jnp.where(both(bottom, last), k, evenly)
+        turned = jnp.where(k < 2, k, jnp.where(k < 4, express + k - 2, k - 2))
+        return jnp.where(both(bottom, last), turned, evenly)
 
     def pass_late(k):
         @pl.when(has2)
@@ -449,6 +470,10 @@
         @pl.when(both(rounds, k == 1))
         def _():
             pass_round(half - 1)
+
+        @pl.when(both(descends, either(k == 1, k == 3)))
+        def _():
+            pass_down(half + 2 + lax.div(k, 2))
 
         @pl.when(k + 1 < heads)
         def _():
@@ -509,7 +534,11 @@
         def _():
             send_next(j).wait_send()
 
-        @pl.when(either(both(rounds, j < half), both(turns_on, j >= half)))
+        @pl.when(both(descends, j >= half))
+        def _():
+            send_down(j).wait_send()
+
+        @pl.when(either(both(rounds, j < half), turns_on(j)))
         def _():
             send_round(j).wait_send()
 

time: 59.6 us -> 55.3 us (0.928)
  the two profiles are of different devices: /device:TPU:193 before, /device:TPU:127 now
where the time goes in v5:
time: 55.3 us; the launch traced here: 55.1 us
  Pallas kernels  54 us (98%)
  local copies, waits for them, and re-layouts  1.15 us (2%)
    pallas_call x1, Pallas kernels, shards(): pl.pallas_call(functools.partial(attention_kernel, sections, rows, heads)...  54 us
    unnamed x1, local copies, waits for them, and re-layouts  1.15 us

profile of v5, /device:TPU:127, one launch (start us, length us, event | category | flops | bytes accessed | tf_op | source)
XLA Modules:
  0.0 55.1 jit_solution(3242315281806452713)
XLA Ops:
  0.0 54.0 %shard_map.46 = bf16[256,3072]{1,0:T(8,128)(2,1)S(1)} custom-call(bf16[256,3072]{1,0:T(8,128)(2,1)} %q_hbm.1, bf16[256,1024]{1,0:T(8,128)(2,1)} %k_hbm.1, bf16[256,1024]{1,0:T(8,128)(2,1)} %v_hbm.1, s32[512,128]{1,0:T(8,128)} %bitcast.1), custom_call_target="tpu_custom_call" | custom-call | tf_op jit(solution)/shard_map/pallas_call | solution.py:553
  54.0 1.1 %copy.6 = bf16[256,3072]{1,0:T(8,128)(2,1)} copy(bf16[256,3072]{1,0:T(8,128)(2,1)S(1)} %shard_map.46) | data formatting | bytes 3145728

commit v6 on v5

--- a/solution.py
+++ b/solution.py
@@ -24,7 +24,7 @@
 def attention_kernel(
     sections, rows, heads,
     q_hbm, k_hbm, v_hbm, docs_hbm, out_hbm,
-    kv, q, onehot, away, docs, stat_max, acc, out,
+    kv, q, onehot, away, docs, stat_max, acc, out, held0, held1,
     send_sem, recv_sem, q_sem, kv_sem, doc_sem, out_sem,
 ):
     half = heads // 2
@@ -317,18 +317,23 @@
         stat_max[j, r] = top
         acc[j, r] = weigh(parts, wide(top), early, j)
 
-    def all_scores(blocks, j):
+    def score(blocks, j, held):
         query = jnp.concatenate([query_of(j, r) for r in range(GROUP)], axis=0)
-        whole = [scores(query, key) for key in [keys_of(block, j) for block in blocks]]
-        return [[part[r * rows:(r + 1) * rows] for part in whole] for r in range(GROUP)]
-
-    def fold_early(j):
-        for r, parts in enumerate(all_scores(early, j)):
-            finish_early(j, r, parts)
-
-    def fold_late(j):
-        for r, parts in enumerate(all_scores(late, j)):
-            finish_late(j, r, parts)
+        for at, block in enumerate(blocks):
+            held[:, at * rows:(at + 1) * rows] = scores(query, keys_of(block, j))
+
+    def parts_of(blocks, r, held):
+        return [
+            held[r * rows:(r + 1) * rows, at * rows:(at + 1) * rows] for at in range(len(blocks))
+        ]
+
+    def fold_early(j, held):
+        for r in range(GROUP):
+            finish_early(j, r, parts_of(early, r, held))
+
+    def fold_late(j, held):
+        for r in range(GROUP):
+            finish_late(j, r, parts_of(late, r, held))
 
     def store_out(h):
         at = pl.ds(pl.multiple_of(h * HEAD_DIM, HEAD_DIM), HEAD_DIM)
@@ -406,8 +411,7 @@
         def _():
             arrived(BACK3 + other, j)
 
-    @pl.loop(0, heads + 3)
-    def _(step):
+    def move(step):
         @pl.when(step < heads)
         def _():
             pass_relay(step)
@@ -445,16 +449,40 @@
         def _():
             pass_down(half + step - (heads + 1))
 
-        @pl.when(step >= 3)
-        def _():
-            early_ready(step - 3)
-            fold_early(step - 3)
+    buffers = (held0, held1)
+
+    @pl.loop(0, (heads + 4) // 2)
+    def _(pair):
+        for side in range(2):
+            step = 2 * pair + side
+            now, before = buffers[side], buffers[1 - side]
+            move(step)
+
+            @pl.when(both(step >= 3, step < heads + 3))
+            def _():
+                early_ready(step - 3)
+
+            @pl.when(step == 3)
+            def _():
+                score(early, step - 3, now)
+
+            @pl.when(both(step > 3, step < heads + 3))
+            def _():
+                score(early, step - 3, now)
+                fold_early(step - 4, before)
+
+            @pl.when(step == heads + 3)
+            def _():
+                fold_early(step - 4, before)
 
     def late_head(k):
         odd = lax.rem(k, 2)
         evenly = half * odd + lax.div(k, 2)
         turned = jnp.where(k < 2, k, jnp.where(k < 4, express + k - 2, k - 2))
-        return jnp.where(both(bottom, last), turned, evenly)
+        mixed = jnp.where(odd == 1, lax.div(k + 1, 2), half - 1 + lax.div(k, 2))
+        delayed = jnp.where(k == 0, 0, jnp.where(k == heads - 1, k, mixed))
+        waits_down = both(last, up_open, lax.rem(s, RING * RING) >= RING * (RING - 1))
+        return jnp.where(both(bottom, last), turned, jnp.where(waits_down, delayed, evenly))
 
     def pass_late(k):
         @pl.when(has2)
@@ -463,31 +491,51 @@
             arrived(BACK2 + c, j)
             send_side(SIDE2, j, BACK2).start()
 
-    pass_late(0)
-
-    @pl.loop(0, heads)
-    def _(k):
-        @pl.when(both(rounds, k == 1))
-        def _():
-            pass_round(half - 1)
-
-        @pl.when(both(descends, either(k == 1, k == 3)))
-        def _():
-            pass_down(half + 2 + lax.div(k, 2))
+    def late_ready(k):
+        @pl.when(has2)
+        def _():
+            arrived(BACK2 + other, late_head(k))
+
+    def move_late(k):
+        @pl.when(both(descends, k == 1))
+        def _():
+            pass_down(heads - 1)
 
         @pl.when(k + 1 < heads)
         def _():
             pass_late(k + 1)
 
-        j = late_head(k)
-
-        @pl.when(has2)
-        def _():
-            arrived(BACK2 + other, j)
-
-        fold_late(j)
+    def store_head(j):
         for r in range(GROUP):
             store_out(j * GROUP + r).start()
+
+    pass_late(0)
+
+    @pl.loop(0, heads // 2)
+    def _(pair):
+        for side in range(2):
+            k = 2 * pair + side
+            now, before = buffers[side], buffers[1 - side]
+            move_late(k)
+            late_ready(k)
+
+            if side == 0:
+                @pl.when(pair == 0)
+                def _():
+                    score(late, late_head(k), now)
+
+                @pl.when(pair > 0)
+                def _():
+                    score(late, late_head(k), now)
+                    fold_late(late_head(k - 1), before)
+                    store_head(late_head(k - 1))
+            else:
+                score(late, late_head(k), now)
+                fold_late(late_head(k - 1), before)
+                store_head(late_head(k - 1))
+
+    fold_late(late_head(heads - 1), buffers[1])
+    store_head(late_head(heads - 1))
 
     @pl.loop(0, heads)
     def _(j):
@@ -564,6 +612,8 @@
             pltpu.VMEM((heads, GROUP, rows, LANES), jnp.float32),
             pltpu.VMEM((heads, GROUP, rows, 2 * HEAD_DIM), jnp.float32),
             pltpu.VMEM((heads * GROUP, rows, HEAD_DIM), jnp.bfloat16),
+            pltpu.VMEM((GROUP * rows, 6 * rows), jnp.float32),
+            pltpu.VMEM((GROUP * rows, 6 * rows), jnp.float32),
             pltpu.SemaphoreType.DMA((KINDS, heads)),
             pltpu.SemaphoreType.DMA((BLOCKS, heads)),
             pltpu.SemaphoreType.DMA((heads * GROUP,)),

time: 55.3 us -> 53.7 us (0.971)
  Pallas kernels: 54 us -> 52.4 us
    pallas_call x1, Pallas kernels: 54 us -> 52.4 us  [shards(): pl.pallas_call(functools.partial(attention_kernel, sections, rows, heads)...]
where the time goes in v6:
time: 53.7 us; the launch traced here: 53.5 us
  Pallas kernels  52.4 us (98%)
  local copies, waits for them, and re-layouts  1.15 us (2%)
    pallas_call x1, Pallas kernels, shards(): pl.pallas_call(functools.partial(attention_kernel, sections, rows, heads)...  52.4 us
    unnamed x1, local copies, waits for them, and re-layouts  1.15 us

profile of v6, /device:TPU:127, one launch (start us, length us, event | category | flops | bytes accessed | tf_op | source)
XLA Modules:
  0.0 53.5 jit_solution(5109139072129139376)
XLA Ops:
  0.0 52.4 %shard_map.46 = bf16[256,3072]{1,0:T(8,128)(2,1)S(1)} custom-call(bf16[256,3072]{1,0:T(8,128)(2,1)} %q_hbm.1, bf16[256,1024]{1,0:T(8,128)(2,1)} %k_hbm.1, bf16[256,1024]{1,0:T(8,128)(2,1)} %v_hbm.1, s32[512,128]{1,0:T(8,128)} %bitcast.1), custom_call_target="tpu_custom_call" | custom-call | tf_op jit(solution)/shard_map/pallas_call | solution.py:601
  52.4 1.1 %copy.6 = bf16[256,3072]{1,0:T(8,128)(2,1)} copy(bf16[256,3072]{1,0:T(8,128)(2,1)S(1)} %shard_map.46) | data formatting | bytes 3145728

commit v7 on v6

--- a/solution.py
+++ b/solution.py
@@ -416,10 +416,6 @@
         def _():
             pass_relay(step)
 
-        @pl.when(both(step >= 2, step < heads + 2))
-        def _():
-            pass_aside(step - 2)
-
         sending, low, high = next_range(step)
 
         @pl.when(sending)
@@ -441,11 +437,11 @@
         def _():
             pass_round(step)
 
-        @pl.when(both(rounds, step >= heads))
+        @pl.when(both(rounds, step >= heads, step < heads + 3))
         def _():
             pass_round(step - heads)
 
-        @pl.when(both(descends, step > heads))
+        @pl.when(both(descends, step > heads, step < heads + 3))
         def _():
             pass_down(half + step - (heads + 1))
 
@@ -458,22 +454,26 @@
             now, before = buffers[side], buffers[1 - side]
             move(step)
 
-            @pl.when(both(step >= 3, step < heads + 3))
+            @pl.when(both(step >= 2, step < heads + 2))
             def _():
-                early_ready(step - 3)
-
-            @pl.when(step == 3)
+                early_ready(step - 2)
+
+            @pl.when(step == 2)
             def _():
-                score(early, step - 3, now)
-
-            @pl.when(both(step > 3, step < heads + 3))
+                score(early, step - 2, now)
+
+            @pl.when(both(step > 2, step < heads + 2))
             def _():
-                score(early, step - 3, now)
-                fold_early(step - 4, before)
-
-            @pl.when(step == heads + 3)
+                score(early, step - 2, now)
+                fold_early(step - 3, before)
+
+            @pl.when(step == heads + 2)
             def _():
-                fold_early(step - 4, before)
+                fold_early(step - 3, before)
+
+            @pl.when(both(step >= 1, step <= heads))
+            def _():
+                pass_aside(step - 1)
 
     def late_head(k):
         odd = lax.rem(k, 2)
@@ -497,9 +497,13 @@
             arrived(BACK2 + other, late_head(k))
 
     def move_late(k):
-        @pl.when(both(descends, k == 1))
-        def _():
-            pass_down(heads - 1)
+        @pl.when(both(rounds, k == 1))
+        def _():
+            pass_round(half - 1)
+
+        @pl.when(both(descends, either(k == 2, k == 4)))
+        def _():
+            pass_down(half + 1 + lax.div(k, 2))
 
         @pl.when(k + 1 < heads)
         def _():

time: 53.7 us -> 57.3 us (1.067)
  Pallas kernels: 52.4 us -> 56 us
    pallas_call x1, Pallas kernels: 52.4 us -> 56 us  [shards(): pl.pallas_call(functools.partial(attention_kernel, sections, rows, heads)...]
where the time goes in v7:
time: 57.3 us; the launch traced here: 57.2 us
  Pallas kernels  56 us (98%)
  local copies, waits for them, and re-layouts  1.15 us (2%)
    pallas_call x1, Pallas kernels, shards(): pl.pallas_call(functools.partial(attention_kernel, sections, rows, heads)...  56 us

profile of v7, /device:TPU:127, one launch (start us, length us, event | category | flops | bytes accessed | tf_op | source)
XLA Modules:
  0.0 57.2 jit_solution(12628827408358297336)
XLA Ops:
  0.0 56.0 %shard_map.46 = bf16[256,3072]{1,0:T(8,128)(2,1)S(1)} custom-call(bf16[256,3072]{1,0:T(8,128)(2,1)} %q_hbm.1, bf16[256,1024]{1,0:T(8,128)(2,1)} %k_hbm.1, bf16[256,1024]{1,0:T(8,128)(2,1)} %v_hbm.1, s32[512,128]{1,0:T(8,128)} %bitcast.1), custom_call_target="tpu_custom_call" | custom-call | tf_op jit(solution)/shard_map/pallas_call | solution.py:605
  56.0 1.1 %copy.6 = bf16[256,3072]{1,0:T(8,128)(2,1)} copy(bf16[256,3072]{1,0:T(8,128)(2,1)S(1)} %shard_map.46) | data formatting | bytes 3145728

commit v8 on v6

--- a/solution.py
+++ b/solution.py
@@ -36,8 +36,12 @@
     first, last = x == 0, x == RING - 1
     top, bottom = s < RING, s >= sections - RING
     below = jnp.logical_not(top)
-    from_left = jnp.where(jnp.logical_and(bottom, x == 2), heads - 2, half)
     crossing = jnp.logical_and(lax.rem(s, RING * RING) < RING, below)
+    before_crossing = lax.rem(s, RING * RING) >= RING * (RING - 1)
+    from_left = jnp.where(
+        x == 2, jnp.where(bottom, heads - 2, jnp.where(before_crossing, half + 1, half)), half
+    )
+    from_right = jnp.where(jnp.logical_and(first, crossing), half + 1, half)
     express = heads - 2
 
     right = row_start + lax.rem(x + 1, RING)
@@ -428,7 +432,7 @@
             def _(j):
                 send_next(j).start()
 
-        @pl.when(both(sends_prev, step >= half + 2, step < heads + 2))
+        @pl.when(both(sends_prev, step >= from_right + 2, step < heads + 2))
         def _():
             send_prev(step - 2).start()
 
@@ -447,7 +451,7 @@
 
         @pl.when(both(descends, step > heads))
         def _():
-            pass_down(half + step - (heads + 1))
+            pass_down(half + step - heads)
 
     buffers = (held0, held1)
 
@@ -479,9 +483,9 @@
         odd = lax.rem(k, 2)
         evenly = half * odd + lax.div(k, 2)
         turned = jnp.where(k < 2, k, jnp.where(k < 4, express + k - 2, k - 2))
-        mixed = jnp.where(odd == 1, lax.div(k + 1, 2), half - 1 + lax.div(k, 2))
-        delayed = jnp.where(k == 0, 0, jnp.where(k == heads - 1, k, mixed))
-        waits_down = both(last, up_open, lax.rem(s, RING * RING) >= RING * (RING - 1))
+        mixed = jnp.where(odd == 1, half + 1 + lax.div(k - 3, 2), lax.div(k, 2) + 1)
+        delayed = jnp.where(k < 3, k, mixed)
+        waits_down = both(last, up_open, before_crossing)
         return jnp.where(both(bottom, last), turned, jnp.where(waits_down, delayed, evenly))
 
     def pass_late(k):
@@ -497,10 +501,6 @@
             arrived(BACK2 + other, late_head(k))
 
     def move_late(k):
-        @pl.when(both(descends, k == 1))
-        def _():
-            pass_down(heads - 1)
-
         @pl.when(k + 1 < heads)
         def _():
             pass_late(k + 1)
@@ -582,7 +582,7 @@
         def _():
             send_next(j).wait_send()
 
-        @pl.when(both(descends, j >= half))
+        @pl.when(both(descends, j > half))
         def _():
             send_down(j).wait_send()
 
@@ -590,7 +590,7 @@
         def _():
             send_round(j).wait_send()
 
-        @pl.when(both(sends_prev, j >= half))
+        @pl.when(both(sends_prev, j >= from_right))
         def _():
             send_prev(j).wait_send()
 

time: 53.7 us -> 52.9 us (0.985); the launches traced: 53.5 us -> 52 us
  Pallas kernels: 52.4 us -> 50.9 us
    pallas_call x1, Pallas kernels: 52.4 us -> 50.9 us  [shards(): pl.pallas_call(functools.partial(attention_kernel, sections, rows, heads)...]
where the time goes in v8:
time: 52.9 us; the launch traced here: 52 us
  Pallas kernels  50.9 us (96%)
  local copies, waits for them, and re-layouts  1.15 us (2%)
    pallas_call x1, Pallas kernels, shards(): pl.pallas_call(functools.partial(attention_kernel, sections, rows, heads)...  50.9 us
    unnamed x1, local copies, waits for them, and re-layouts  1.15 us

profile of v8, /device:TPU:127, one launch (start us, length us, event | category | flops | bytes accessed | tf_op | source)
XLA Modules:
  0.0 52.0 jit_solution(15915515436954532109)
XLA Ops:
  0.0 50.9 %shard_map.46 = bf16[256,3072]{1,0:T(8,128)(2,1)S(1)} custom-call(bf16[256,3072]{1,0:T(8,128)(2,1)} %q_hbm.1, bf16[256,1024]{1,0:T(8,128)(2,1)} %k_hbm.1, bf16[256,1024]{1,0:T(8,128)(2,1)} %v_hbm.1, s32[512,128]{1,0:T(8,128)} %bitcast.1), custom_call_target="tpu_custom_call" | custom-call | tf_op jit(solution)/shard_map/pallas_call | solution.py:601
  50.9 1.1 %copy.6 = bf16[256,3072]{1,0:T(8,128)(2,1)} copy(bf16[256,3072]{1,0:T(8,128)(2,1)S(1)} %shard_map.46) | data formatting | bytes 3145728

commit v9 on v8

--- a/solution.py
+++ b/solution.py
@@ -449,9 +449,9 @@
         def _():
             pass_round(step - heads)
 
-        @pl.when(both(descends, step > heads))
-        def _():
-            pass_down(half + step - heads)
+        @pl.when(both(descends, step > heads + 1))
+        def _():
+            pass_down(half + step - (heads + 1))
 
     buffers = (held0, held1)
 
@@ -501,6 +501,10 @@
             arrived(BACK2 + other, late_head(k))
 
     def move_late(k):
+        @pl.when(both(descends, k == 0))
+        def _():
+            pass_down(heads - 1)
+
         @pl.when(k + 1 < heads)
         def _():
             pass_late(k + 1)

time: 52.9 us -> 53.6 us (1.013); the launches traced: 52 us -> 53.4 us
  Pallas kernels: 50.9 us -> 52.3 us
    pallas_call x1, Pallas kernels: 50.9 us -> 52.3 us  [shards(): pl.pallas_call(functools.partial(attention_kernel, sections, rows, heads)...]
where the time goes in v9:
time: 53.6 us; the launch traced here: 53.4 us
  Pallas kernels  52.3 us (98%)
  local copies, waits for them, and re-layouts  1.15 us (2%)
    pallas_call x1, Pallas kernels, shards(): pl.pallas_call(functools.partial(attention_kernel, sections, rows, heads)...  52.3 us
    unnamed x1, local copies, waits for them, and re-layouts  1.15 us

profile of v9, /device:TPU:127, one launch (start us, length us, event | category | flops | bytes accessed | tf_op | source)
XLA Modules:
  0.0 53.4 jit_solution(11420995202268962243)
XLA Ops:
  0.0 52.3 %shard_map.46 = bf16[256,3072]{1,0:T(8,128)(2,1)S(1)} custom-call(bf16[256,3072]{1,0:T(8,128)(2,1)} %q_hbm.1, bf16[256,1024]{1,0:T(8,128)(2,1)} %k_hbm.1, bf16[256,1024]{1,0:T(8,128)(2,1)} %v_hbm.1, s32[512,128]{1,0:T(8,128)} %bitcast.1), custom_call_target="tpu_custom_call" | custom-call | tf_op jit(solution)/shard_map/pallas_call | solution.py:605
  52.3 1.1 %copy.6 = bf16[256,3072]{1,0:T(8,128)(2,1)} copy(bf16[256,3072]{1,0:T(8,128)(2,1)S(1)} %shard_map.46) | data formatting | bytes 3145728

commit v10 on v9

--- a/solution.py
+++ b/solution.py
@@ -449,9 +449,9 @@
         def _():
             pass_round(step - heads)
 
-        @pl.when(both(descends, step > heads + 1))
-        def _():
-            pass_down(half + step - (heads + 1))
+        @pl.when(both(descends, step > heads, step < heads + 3))
+        def _():
+            pass_down(half + step - heads)
 
     buffers = (held0, held1)
 

time: 53.6 us -> 52.4 us (0.978)
  Pallas kernels: 52.3 us -> 50.9 us
    pallas_call x1, Pallas kernels: 52.3 us -> 50.9 us  [shards(): pl.pallas_call(functools.partial(attention_kernel, sections, rows, heads)...]
where the time goes in v10:
time: 52.4 us; the launch traced here: 52 us
  Pallas kernels  50.9 us (97%)
  local copies, waits for them, and re-layouts  1.15 us (2%)
    pallas_call x1, Pallas kernels, shards(): pl.pallas_call(functools.partial(attention_kernel, sections, rows, heads)...  50.9 us
    unnamed x1, local copies, waits for them, and re-layouts  1.15 us

profile of v10, /device:TPU:127, one launch (start us, length us, event | category | flops | bytes accessed | tf_op | source)
XLA Modules:
  0.0 52.0 jit_solution(16111366949733199045)
XLA Ops:
  0.0 50.9 %shard_map.46 = bf16[256,3072]{1,0:T(8,128)(2,1)S(1)} custom-call(bf16[256,3072]{1,0:T(8,128)(2,1)} %q_hbm.1, bf16[256,1024]{1,0:T(8,128)(2,1)} %k_hbm.1, bf16[256,1024]{1,0:T(8,128)(2,1)} %v_hbm.1, s32[512,128]{1,0:T(8,128)} %bitcast.1), custom_call_target="tpu_custom_call" | custom-call | tf_op jit(solution)/shard_map/pallas_call | solution.py:605
  50.9 1.1 %copy.6 = bf16[256,3072]{1,0:T(8,128)(2,1)} copy(bf16[256,3072]{1,0:T(8,128)(2,1)S(1)} %shard_map.46) | data formatting | bytes 3145728
